TPU v7x, 32 devices: a whole 2x2x4 slice. The times are simulated.
32 devices in a mesh: cell: 2 (over core), gene: 4 (over y, x), rank: 4 (over z).
Axes of the slice: x: 2, y: 2, z: 4, core: 2. Of those that a mesh axis runs over, the one named last changes fastest.
Arguments:
- blocks: bfloat16 [2, 16, 96, 256, 128], P('cell', ('gene', 'rank')), may hold values from -6 to 6
- block_pos: int32 [2, 16, 96], P('cell', ('gene', 'rank')), may hold values from 0 to 127, as said below
- block_count: int32 [2, 16], P('cell', ('gene', 'rank')), may hold values from 32 to 96, as said below
- test_right: bfloat16 [32768, 512], P(('gene', 'rank')), may hold values from -0.0625 to 0.0625
- test_left: bfloat16 [4096, 768], P('cell', 'rank'), may hold values from -0.1875 to 0.1875
- gene_sketch_old: float32 [768, 32768], P('cell', ('gene', 'rank')), may hold values from -4 to 4
Outputs:
- right_sketch: float32 [4096, 512], P(('cell', 'gene', 'rank'))
- gene_sketch: float32 [768, 32768], P('cell', ('gene', 'rank'))
- core: float32 [768, 512], P('cell')
Inputs may be any that keep to these rules, and one draw needn't show every extreme that they name: `block_pos`: position p names row block p // 16 and gene block p % 16 of the device's tile; the 96 positions of one device are distinct. `block_count`: some device has all 96 slots live in every draw; slots from the count on are not part of A.
All inputs are finite; a program needn't handle non-finite values.
Results may differ from a plain program's by a relative error of at most 0.0003.
Values may be sent and summed in bfloat16 or wider, within the bound.
A program may use at most 128 MiB of HBM per device.

v0:
```python
import jax
import jax.numpy as jnp
from jax import lax
from jax.sharding import PartitionSpec as P

GROUP = 16


def body(blocks, block_pos, block_count, test_right, test_left, gene_sketch_old):
    highest = lax.Precision.HIGHEST
    tiles = blocks[0, 0]
    positions = block_pos[0, 0]
    live_count = block_count[0, 0]
    slots, block_rows, block_cols = tiles.shape
    gene_blocks = test_right.shape[0] // block_cols
    right_width = test_right.shape[1]
    left_full = lax.all_gather(test_left, "rank", axis=1, tiled=True)
    row_blocks = left_full.shape[0] // block_rows
    left_width = left_full.shape[1]
    right_table = test_right.reshape(gene_blocks, block_cols, right_width)
    left_table = left_full.reshape(row_blocks, block_rows, left_width)
    offsets = jnp.arange(GROUP, dtype=jnp.int32)

    def visit(turn_index, carry):
        right_acc, gene_acc = carry
        first_slot = turn_index * GROUP
        group_tiles = lax.dynamic_slice_in_dim(tiles, first_slot, GROUP, 0)
        group_places = lax.dynamic_slice_in_dim(positions, first_slot, GROUP, 0)
        alive_mask = (first_slot + offsets < live_count).astype(jnp.float32)
        row_block = group_places // gene_blocks
        gene_block = group_places % gene_blocks
        right_rows = jnp.take(right_table, gene_block, axis=0)
        left_rows = jnp.take(left_table, row_block, axis=0)
        right_terms = (
            jnp.einsum("pik,pkr->pir", group_tiles, right_rows, preferred_element_type=jnp.float32)
            * alive_mask[:, None, None]
        )
        gene_terms = (
            jnp.einsum("pil,pik->lpk", left_rows, group_tiles, preferred_element_type=jnp.float32)
            * alive_mask[None, :, None]
        )
        right_acc = right_acc.at[row_block].add(right_terms)
        gene_acc = gene_acc.at[:, gene_block].add(gene_terms)
        return (right_acc, gene_acc)

    turn_count = (live_count + GROUP - 1) // GROUP
    initial = (
        jnp.zeros((row_blocks, block_rows, right_width), jnp.float32),
        jnp.zeros((left_width, gene_blocks, block_cols), jnp.float32),
    )
    right_part, gene_part = lax.fori_loop(0, turn_count, visit, initial)
    right_flat = right_part.reshape(row_blocks * block_rows, right_width)
    gene_flat = gene_part.reshape(left_width, gene_blocks * block_cols)
    right_half = lax.psum_scatter(right_flat, "gene", scatter_dimension=0, tiled=True)
    right_mine = lax.psum_scatter(right_half, "rank", scatter_dimension=0, tiled=True)
    gene_mine = lax.psum_scatter(gene_flat, "cell", scatter_dimension=0, tiled=True)
    gene_sketch = gene_sketch_old + gene_mine
    shard_index = lax.axis_index("gene") * lax.axis_size("rank") + lax.axis_index("rank")
    mine_rows = right_mine.shape[0]
    left_mine = lax.dynamic_slice_in_dim(left_full, shard_index * mine_rows, mine_rows, 0).astype(
        jnp.float32
    )
    core_part = lax.dot_general(left_mine, right_mine, (((0,), (0,)), ((), ())), precision=highest)
    core_total = lax.psum(core_part, ("cell", "gene", "rank"))
    share = left_width // lax.axis_size("cell")
    core = lax.dynamic_slice_in_dim(core_total, lax.axis_index("cell") * share, share, 0)
    return (right_mine, gene_sketch, core)


def solution(mesh):
    return jax.shard_map(
        body,
        mesh=mesh,
        in_specs=(
            P("cell", ("gene", "rank"), None, None, None),
            P("cell", ("gene", "rank"), None),
            P("cell", ("gene", "rank")),
            P(("gene", "rank"), None),
            P("cell", "rank"),
            P("cell", ("gene", "rank")),
        ),
        out_specs=(P(("cell", "gene", "rank"), None), P("cell", ("gene", "rank")), P("cell", None)),
        check_vma=False,
    )
```

profile of v0, /device:TPU:1, one launch (start us, length us, event | category | flops | bytes accessed | tf_op | source)
XLA Modules:
  0.0 695.8 jit_solution(15199658908383752672)
XLA Ops:
  8.6 66.3 %all-gather.2.cloned.1.call-done = bf16[2048,768]{0,1:T(8,128)(2,1)} async-done(((bf16[2048,192]{0,1:T(8,128)(2,1)}), bf16[2048,768]{0,1:T(8,128)(2,1)}) %all-gather.2.cloned.1.call-update) | async-done | bytes 3145744 | tf_op jit(solution)/shard_map/all_gather | solution.py:17
  84.0 305.6 %while.15 = (s32[]{:T(128)}, f32[8,256,512]{2,1,0:T(8,128)}, f32[768,16,128]{2,0,1:T(8,128)}, s32[]{:T(128)}, s32[96]{0:T(128)S(1)}, /*index=5*/bf16[96,256,128]...) while((s32[]{:T(128)}, f32[8,256,512]{2,1,0:T(8,128)}, ...), condition=%wide.region_3.4_spmd.clone, body=%wide.region_0.3_spmd.clone.sunk | while | flops 1353714176 | bytes 98575488 | solution.py:51
  88.3 7.2 %multiply_bitcast_fusion.2 = f32[16,768,128]{1,2,0:T(8,128)} fusion(f32[16]{0:T(128)S(1)} %get-tuple-element.245, bf16[16,256,768]{2,1,0:T(8,128)(2,1)} %gather_fusion.1, pred[16]{0:T(512)(128)(4,1)S(1)} %get-tuple-element.249, bf16[96,256,128]{2,1,0:T(8,128)(2,1)} %get-tuple-element.281, s32[]{:T(128)S(6)} %select_n.101), kind=kOutput, calls=%fused_computation.5.clone.1 | convolution fusion | flops 810024960 | bytes 13631572 | tf_op jit(solution)/shard_map/while/body/pil,pik->lpk/dot_general | solution.py:39
  95.5 6.5 copy.17
  102.0 15.0 %scatter_fusion.1 = f32[768,16,128]{2,0,1:T(8,128)} fusion(f32[768,16,128]{2,0,1:T(8,128)} %get-tuple-element.265, s32[16]{0:T(128)S(1)} %get-tuple-element.247, f32[16,768,128]{2,1,0:T(8,128)} %copy.17), kind=kCustom, calls=%fused_computation.3.clone.clone.1 | custom fusion | flops 1572864 | bytes 18874432 | tf_op jit(solution)/shard_map/while/body/scatter-add | solution.py:43
  127.1 18.1 %scatter_fusion = f32[8,256,512]{2,1,0:T(8,128)} fusion(f32[8,256,512]{2,1,0:T(8,128)} %get-tuple-element.264, s32[16]{0:T(128)S(1)} %get-tuple-element.244, f32[16,256,512]{2,1,0:T(8,128)} %broadcast_multiply_fusion.2), kind=kCustom, calls=%fused_computation.2.clone.clone.1 | custom fusion | flops 2097152 | bytes 25165888 | tf_op jit(solution)/shard_map/while/body/scatter-add | solution.py:42
  149.4 7.2 %multiply_bitcast_fusion.2 = f32[16,768,128]{1,2,0:T(8,128)} fusion(f32[16]{0:T(128)S(1)} %get-tuple-element.245, bf16[16,256,768]{2,1,0:T(8,128)(2,1)} %gather_fusion.1, pred[16]{0:T(512)(128)(4,1)S(1)} %get-tuple-element.249, bf16[96,256,128]{2,1,0:T(8,128)(2,1)} %get-tuple-element.281, s32[]{:T(128)S(6)} %select_n.101), kind=kOutput, calls=%fused_computation.5.clone.1 | convolution fusion | flops 810024960 | bytes 13631572 | tf_op jit(solution)/shard_map/while/body/pil,pik->lpk/dot_general | solution.py:39
  156.6 6.5 copy.17
  163.2 15.3 %scatter_fusion.1 = f32[768,16,128]{2,0,1:T(8,128)} fusion(f32[768,16,128]{2,0,1:T(8,128)} %get-tuple-element.265, s32[16]{0:T(128)S(1)} %get-tuple-element.247, f32[16,768,128]{2,1,0:T(8,128)} %copy.17), kind=kCustom, calls=%fused_computation.3.clone.clone.1 | custom fusion | flops 1572864 | bytes 18874432 | tf_op jit(solution)/shard_map/while/body/scatter-add | solution.py:43
  188.5 18.0 %scatter_fusion = f32[8,256,512]{2,1,0:T(8,128)} fusion(f32[8,256,512]{2,1,0:T(8,128)} %get-tuple-element.264, s32[16]{0:T(128)S(1)} %get-tuple-element.244, f32[16,256,512]{2,1,0:T(8,128)} %broadcast_multiply_fusion.2), kind=kCustom, calls=%fused_computation.2.clone.clone.1 | custom fusion | flops 2097152 | bytes 25165888 | tf_op jit(solution)/shard_map/while/body/scatter-add | solution.py:42
  210.8 7.2 %multiply_bitcast_fusion.2 = f32[16,768,128]{1,2,0:T(8,128)} fusion(f32[16]{0:T(128)S(1)} %get-tuple-element.245, bf16[16,256,768]{2,1,0:T(8,128)(2,1)} %gather_fusion.1, pred[16]{0:T(512)(128)(4,1)S(1)} %get-tuple-element.249, bf16[96,256,128]{2,1,0:T(8,128)(2,1)} %get-tuple-element.281, s32[]{:T(128)S(6)} %select_n.101), kind=kOutput, calls=%fused_computation.5.clone.1 | convolution fusion | flops 810024960 | bytes 13631572 | tf_op jit(solution)/shard_map/while/body/pil,pik->lpk/dot_general | solution.py:39
  218.0 6.5 copy.17
  224.6 14.9 %scatter_fusion.1 = f32[768,16,128]{2,0,1:T(8,128)} fusion(f32[768,16,128]{2,0,1:T(8,128)} %get-tuple-element.265, s32[16]{0:T(128)S(1)} %get-tuple-element.247, f32[16,768,128]{2,1,0:T(8,128)} %copy.17), kind=kCustom, calls=%fused_computation.3.clone.clone.1 | custom fusion | flops 1572864 | bytes 18874432 | tf_op jit(solution)/shard_map/while/body/scatter-add | solution.py:43
  249.6 18.0 %scatter_fusion = f32[8,256,512]{2,1,0:T(8,128)} fusion(f32[8,256,512]{2,1,0:T(8,128)} %get-tuple-element.264, s32[16]{0:T(128)S(1)} %get-tuple-element.244, f32[16,256,512]{2,1,0:T(8,128)} %broadcast_multiply_fusion.2), kind=kCustom, calls=%fused_computation.2.clone.clone.1 | custom fusion | flops 2097152 | bytes 25165888 | tf_op jit(solution)/shard_map/while/body/scatter-add | solution.py:42
  271.9 7.2 %multiply_bitcast_fusion.2 = f32[16,768,128]{1,2,0:T(8,128)} fusion(f32[16]{0:T(128)S(1)} %get-tuple-element.245, bf16[16,256,768]{2,1,0:T(8,128)(2,1)} %gather_fusion.1, pred[16]{0:T(512)(128)(4,1)S(1)} %get-tuple-element.249, bf16[96,256,128]{2,1,0:T(8,128)(2,1)} %get-tuple-element.281, s32[]{:T(128)S(6)} %select_n.101), kind=kOutput, calls=%fused_computation.5.clone.1 | convolution fusion | flops 810024960 | bytes 13631572 | tf_op jit(solution)/shard_map/while/body/pil,pik->lpk/dot_general | solution.py:39
  285.6 15.1 %scatter_fusion.1 = f32[768,16,128]{2,0,1:T(8,128)} fusion(f32[768,16,128]{2,0,1:T(8,128)} %get-tuple-element.265, s32[16]{0:T(128)S(1)} %get-tuple-element.247, f32[16,768,128]{2,1,0:T(8,128)} %copy.17), kind=kCustom, calls=%fused_computation.3.clone.clone.1 | custom fusion | flops 1572864 | bytes 18874432 | tf_op jit(solution)/shard_map/while/body/scatter-add | solution.py:43
  310.8 17.6 %scatter_fusion = f32[8,256,512]{2,1,0:T(8,128)} fusion(f32[8,256,512]{2,1,0:T(8,128)} %get-tuple-element.264, s32[16]{0:T(128)S(1)} %get-tuple-element.244, f32[16,256,512]{2,1,0:T(8,128)} %broadcast_multiply_fusion.2), kind=kCustom, calls=%fused_computation.2.clone.clone.1 | custom fusion | flops 2097152 | bytes 25165888 | tf_op jit(solution)/shard_map/while/body/scatter-add | solution.py:42
  332.7 7.2 %multiply_bitcast_fusion.2 = f32[16,768,128]{1,2,0:T(8,128)} fusion(f32[16]{0:T(128)S(1)} %get-tuple-element.245, bf16[16,256,768]{2,1,0:T(8,128)(2,1)} %gather_fusion.1, pred[16]{0:T(512)(128)(4,1)S(1)} %get-tuple-element.249, bf16[96,256,128]{2,1,0:T(8,128)(2,1)} %get-tuple-element.281, s32[]{:T(128)S(6)} %select_n.101), kind=kOutput, calls=%fused_computation.5.clone.1 | convolution fusion | flops 810024960 | bytes 13631572 | tf_op jit(solution)/shard_map/while/body/pil,pik->lpk/dot_general | solution.py:39
  346.4 15.1 %scatter_fusion.1 = f32[768,16,128]{2,0,1:T(8,128)} fusion(f32[768,16,128]{2,0,1:T(8,128)} %get-tuple-element.265, s32[16]{0:T(128)S(1)} %get-tuple-element.247, f32[16,768,128]{2,1,0:T(8,128)} %copy.17), kind=kCustom, calls=%fused_computation.3.clone.clone.1 | custom fusion | flops 1572864 | bytes 18874432 | tf_op jit(solution)/shard_map/while/body/scatter-add | solution.py:43
  371.7 18.0 %scatter_fusion = f32[8,256,512]{2,1,0:T(8,128)} fusion(f32[8,256,512]{2,1,0:T(8,128)} %get-tuple-element.264, s32[16]{0:T(128)S(1)} %get-tuple-element.244, f32[16,256,512]{2,1,0:T(8,128)} %broadcast_multiply_fusion.2), kind=kCustom, calls=%fused_computation.2.clone.clone.1 | custom fusion | flops 2097152 | bytes 25165888 | tf_op jit(solution)/shard_map/while/body/scatter-add | solution.py:42
  389.7 112.0 %reduce-scatter.4.cloned.1.call-done = f32[512,512]{1,0:T(8,128)} async-done(((f32[2048,512]{1,0:T(8,128)}), f32[512,512]{1,0:T(8,128)}) %reduce-scatter.4.cloned.1.call-update) | async-done | bytes 1048592 | tf_op jit(solution)/shard_map/reduce_scatter | solution.py:54
  501.8 29.9 %reduce-scatter.6.cloned.1.call-done = f32[128,512]{1,0:T(8,128)} async-done(((f32[512,512]{1,0:T(8,128)}), f32[128,512]{1,0:T(8,128)}) %reduce-scatter.6.cloned.1.call-update) | async-done | bytes 262160 | tf_op jit(solution)/shard_map/reduce_scatter | solution.py:55
  541.1 126.8 %all-reduce.2.cloned.1.call-done = f32[768,512]{1,0:T(8,128)} async-done(((f32[768,512]{1,0:T(8,128)}), f32[768,512]{1,0:T(8,128)}) %all-reduce.2.cloned.1.call-update) | async-done | bytes 1572880 | tf_op jit(solution)/shard_map/psum | solution.py:64
  670.0 15.3 %reduce-scatter.8.cloned.1.call-done = f32[384,2048]{1,0:T(8,128)} async-done(((f32[768,2048]{1,0:T(8,128)}), f32[384,2048]{1,0:T(8,128)}) %reduce-scatter.8.cloned.1.call-update) | async-done | bytes 3145744 | tf_op jit(solution)/shard_map/reduce_scatter | solution.py:56
  (58 shorter events, 110.3 us)
Async XLA Ops:
  7.2 67.8 %all-gather.2.cloned.1.call-start = ((), (), s32[]{:S(2)}) async-start(), calls=%async_computation.3 | async-start | bytes 3932160 | tf_op jit(solution)/shard_map/all_gather | solution.py:17
  7.9 493.9 %reduce-scatter.4.cloned.1.call-start = ((), (), s32[]{:S(2)}) async-start(), calls=%async_computation.4 | async-start | bytes 5242880 | tf_op jit(solution)/shard_map/reduce_scatter | solution.py:54
  78.1 5.9 copy-start.1
  389.7 142.1 %reduce-scatter.6.cloned.1.call-start = ((), (), s32[]{:S(2)}) async-start(), calls=%async_computation.5 | async-start | bytes 1310720 | tf_op jit(solution)/shard_map/reduce_scatter | solution.py:55
  501.8 166.1 %all-reduce.2.cloned.1.call-start = ((), (), s32[]{:S(2)}) async-start(), calls=%async_computation.7 | async-start | bytes 3145728 | tf_op jit(solution)/shard_map/psum | solution.py:64
  534.7 150.5 %reduce-scatter.8.cloned.1.call-start = ((), (), s32[]{:S(2)}) async-start(), calls=%async_computation.6 | async-start | bytes 9437184 | tf_op jit(solution)/shard_map/reduce_scatter | solution.py:56
  541.1 144.1 %copy-start = (f32[384,2048]{1,0:T(8,128)S(1)}, f32[384,2048]{1,0:T(8,128)}, u32[]{:S(2)}) copy-start(f32[384,2048]{1,0:T(8,128)} %param.13) | copy-start | bytes 9437188
Sparse Core Ops, SparseCore 0:
  9.5 65.3 all-gather.1
  389.8 111.9 reduce-scatter.3
  504.6 27.0 reduce-scatter.5
  537.4 130.4 all-reduce.1
  670.1 15.1 reduce-scatter.7
where the time goes:
time: 697 us; the launch traced here: 696 us
  waiting for transfers between devices  351 us (50%)
  other arithmetic  173 us (25%)
  local copies, waits for them, and re-layouts  85.8 us (12%)
  matrix products  71.3 us (10%)
  between operations  14.5 us (2%)
    psum x1, waiting for transfers between devices, body(): core_total = lax.psum(core_part, ('cell', 'gene', 'rank'))  127 us
    reduce_scatter x1, waiting for transfers between devices, body(): lax.psum_scatter(right_flat, 'gene', scatter_dimension=0, tiled=True)  112 us
    scatter-add x5, other arithmetic, visit(): right_acc = right_acc.at[row_block].add(right_terms)  89.7 us
    scatter-add x5, other arithmetic, visit(): gene_acc = gene_acc.at[:, gene_block].add(gene_terms)  75.5 us
    all_gather x1, waiting for transfers between devices, body(): left_full = lax.all_gather(test_left, 'rank', axis=1, tiled=True)  66.3 us
    dot_general x5, matrix products, visit(): jnp.einsum('pil,pik->lpk', left_rows, group_tiles, preferred_element_type...  35.9 us
    mul x5, local copies, waits for them, and re-layouts, visit(): jnp.einsum('pil,pik->lpk', left_rows, group_tiles, preferred_element_type...  32.7 us
    dot_general x5, matrix products, visit(): jnp.einsum('pik,pkr->pir', group_tiles, right_rows, preferred_element_typ...  32.4 us
  transfers between devices with their start and end apart: 5, of which 5 were waited for; matrix products, arithmetic and copies ran while one was open for 1% of the time, Pallas kernels for 0%

commit v1 on v0

--- a/solution.py
+++ b/solution.py
@@ -61,7 +61,8 @@
         jnp.float32
     )
     core_part = lax.dot_general(left_mine, right_mine, (((0,), (0,)), ((), ())), precision=highest)
-    core_total = lax.psum(core_part, ("cell", "gene", "rank"))
+    half = lax.psum(core_part, ("gene", "rank"))
+    core_total = lax.psum(half, "cell")
     share = left_width // lax.axis_size("cell")
     core = lax.dynamic_slice_in_dim(core_total, lax.axis_index("cell") * share, share, 0)
     return (right_mine, gene_sketch, core)

time: 697 us -> 705 us (1.011)
    psum x1 -> x2, waiting for transfers between devices: 127 us -> 132 us  [the longest x1 112 us: body(): half = lax.psum(core_part, ('gene', 'rank'))]
  transfers between devices with their start and end apart: 5 -> 6, of which waited for: 5 -> 6; matrix products, arithmetic and copies ran while one was open for 1% -> 1% of each run, Pallas kernels for 0% -> 0%
where the time goes in v1:
time: 705 us; the launch traced here: 703 us
  waiting for transfers between devices  358 us (51%)
  other arithmetic  173 us (25%)
  local copies, waits for them, and re-layouts  85.9 us (12%)
  matrix products  71.3 us (10%)
  between operations  14.8 us (2%)
    reduce_scatter x1, waiting for transfers between devices, body(): lax.psum_scatter(right_flat, 'gene', scatter_dimension=0, tiled=True)  112 us
    psum x1, waiting for transfers between devices, body(): half = lax.psum(core_part, ('gene', 'rank'))  112 us
    scatter-add x5, other arithmetic, visit(): right_acc = right_acc.at[row_block].add(right_terms)  89.7 us
    scatter-add x5, other arithmetic, visit(): gene_acc = gene_acc.at[:, gene_block].add(gene_terms)  75.5 us
    all_gather x1, waiting for transfers between devices, body(): left_full = lax.all_gather(test_left, 'rank', axis=1, tiled=True)  66.3 us
    dot_general x5, matrix products, visit(): jnp.einsum('pil,pik->lpk', left_rows, group_tiles, preferred_element_type...  35.9 us
    mul x5, local copies, waits for them, and re-layouts, visit(): jnp.einsum('pil,pik->lpk', left_rows, group_tiles, preferred_element_type...  32.7 us
    dot_general x5, matrix products, visit(): jnp.einsum('pik,pkr->pir', group_tiles, right_rows, preferred_element_typ...  32.4 us
  transfers between devices with their start and end apart: 6, of which 6 were waited for; matrix products, arithmetic and copies ran while one was open for 1% of the time, Pallas kernels for 0%

profile of v1, /device:TPU:1, one launch (start us, length us, event | category | flops | bytes accessed | tf_op | source)
XLA Modules:
  0.0 703.3 jit_solution(18394939870155386839)
XLA Ops:
  8.6 66.3 %all-gather.2.cloned.1.call-done = bf16[2048,768]{0,1:T(8,128)(2,1)} async-done(((bf16[2048,192]{0,1:T(8,128)(2,1)}), bf16[2048,768]{0,1:T(8,128)(2,1)}) %all-gather.2.cloned.1.call-update) | async-done | bytes 3145744 | tf_op jit(solution)/shard_map/all_gather | solution.py:17
  84.0 305.6 %while.15 = (s32[]{:T(128)}, f32[8,256,512]{2,1,0:T(8,128)}, f32[768,16,128]{2,0,1:T(8,128)}, s32[]{:T(128)}, s32[96]{0:T(128)S(1)}, /*index=5*/bf16[96,256,128]...) while((s32[]{:T(128)}, f32[8,256,512]{2,1,0:T(8,128)}, ...), condition=%wide.region_3.4_spmd.clone, body=%wide.region_0.3_spmd.clone.sunk | while | flops 1353714176 | bytes 98575488 | solution.py:51
  88.3 7.2 %multiply_bitcast_fusion.2 = f32[16,768,128]{1,2,0:T(8,128)} fusion(f32[16]{0:T(128)S(1)} %get-tuple-element.245, bf16[16,256,768]{2,1,0:T(8,128)(2,1)} %gather_fusion.1, pred[16]{0:T(512)(128)(4,1)S(1)} %get-tuple-element.249, bf16[96,256,128]{2,1,0:T(8,128)(2,1)} %get-tuple-element.281, s32[]{:T(128)S(6)} %select_n.101), kind=kOutput, calls=%fused_computation.5.clone.1 | convolution fusion | flops 810024960 | bytes 13631572 | tf_op jit(solution)/shard_map/while/body/pil,pik->lpk/dot_general | solution.py:39
  95.5 6.5 copy.17
  102.0 15.0 %scatter_fusion.1 = f32[768,16,128]{2,0,1:T(8,128)} fusion(f32[768,16,128]{2,0,1:T(8,128)} %get-tuple-element.265, s32[16]{0:T(128)S(1)} %get-tuple-element.247, f32[16,768,128]{2,1,0:T(8,128)} %copy.17), kind=kCustom, calls=%fused_computation.3.clone.clone.1 | custom fusion | flops 1572864 | bytes 18874432 | tf_op jit(solution)/shard_map/while/body/scatter-add | solution.py:43
  127.1 18.1 %scatter_fusion = f32[8,256,512]{2,1,0:T(8,128)} fusion(f32[8,256,512]{2,1,0:T(8,128)} %get-tuple-element.264, s32[16]{0:T(128)S(1)} %get-tuple-element.244, f32[16,256,512]{2,1,0:T(8,128)} %broadcast_multiply_fusion.2), kind=kCustom, calls=%fused_computation.2.clone.clone.1 | custom fusion | flops 2097152 | bytes 25165888 | tf_op jit(solution)/shard_map/while/body/scatter-add | solution.py:42
  149.4 7.2 %multiply_bitcast_fusion.2 = f32[16,768,128]{1,2,0:T(8,128)} fusion(f32[16]{0:T(128)S(1)} %get-tuple-element.245, bf16[16,256,768]{2,1,0:T(8,128)(2,1)} %gather_fusion.1, pred[16]{0:T(512)(128)(4,1)S(1)} %get-tuple-element.249, bf16[96,256,128]{2,1,0:T(8,128)(2,1)} %get-tuple-element.281, s32[]{:T(128)S(6)} %select_n.101), kind=kOutput, calls=%fused_computation.5.clone.1 | convolution fusion | flops 810024960 | bytes 13631572 | tf_op jit(solution)/shard_map/while/body/pil,pik->lpk/dot_general | solution.py:39
  156.6 6.5 copy.17
  163.2 15.3 %scatter_fusion.1 = f32[768,16,128]{2,0,1:T(8,128)} fusion(f32[768,16,128]{2,0,1:T(8,128)} %get-tuple-element.265, s32[16]{0:T(128)S(1)} %get-tuple-element.247, f32[16,768,128]{2,1,0:T(8,128)} %copy.17), kind=kCustom, calls=%fused_computation.3.clone.clone.1 | custom fusion | flops 1572864 | bytes 18874432 | tf_op jit(solution)/shard_map/while/body/scatter-add | solution.py:43
  188.5 18.0 %scatter_fusion = f32[8,256,512]{2,1,0:T(8,128)} fusion(f32[8,256,512]{2,1,0:T(8,128)} %get-tuple-element.264, s32[16]{0:T(128)S(1)} %get-tuple-element.244, f32[16,256,512]{2,1,0:T(8,128)} %broadcast_multiply_fusion.2), kind=kCustom, calls=%fused_computation.2.clone.clone.1 | custom fusion | flops 2097152 | bytes 25165888 | tf_op jit(solution)/shard_map/while/body/scatter-add | solution.py:42
  210.8 7.2 %multiply_bitcast_fusion.2 = f32[16,768,128]{1,2,0:T(8,128)} fusion(f32[16]{0:T(128)S(1)} %get-tuple-element.245, bf16[16,256,768]{2,1,0:T(8,128)(2,1)} %gather_fusion.1, pred[16]{0:T(512)(128)(4,1)S(1)} %get-tuple-element.249, bf16[96,256,128]{2,1,0:T(8,128)(2,1)} %get-tuple-element.281, s32[]{:T(128)S(6)} %select_n.101), kind=kOutput, calls=%fused_computation.5.clone.1 | convolution fusion | flops 810024960 | bytes 13631572 | tf_op jit(solution)/shard_map/while/body/pil,pik->lpk/dot_general | solution.py:39
  224.6 14.9 %scatter_fusion.1 = f32[768,16,128]{2,0,1:T(8,128)} fusion(f32[768,16,128]{2,0,1:T(8,128)} %get-tuple-element.265, s32[16]{0:T(128)S(1)} %get-tuple-element.247, f32[16,768,128]{2,1,0:T(8,128)} %copy.17), kind=kCustom, calls=%fused_computation.3.clone.clone.1 | custom fusion | flops 1572864 | bytes 18874432 | tf_op jit(solution)/shard_map/while/body/scatter-add | solution.py:43
  249.6 18.0 %scatter_fusion = f32[8,256,512]{2,1,0:T(8,128)} fusion(f32[8,256,512]{2,1,0:T(8,128)} %get-tuple-element.264, s32[16]{0:T(128)S(1)} %get-tuple-element.244, f32[16,256,512]{2,1,0:T(8,128)} %broadcast_multiply_fusion.2), kind=kCustom, calls=%fused_computation.2.clone.clone.1 | custom fusion | flops 2097152 | bytes 25165888 | tf_op jit(solution)/shard_map/while/body/scatter-add | solution.py:42
  271.9 7.2 %multiply_bitcast_fusion.2 = f32[16,768,128]{1,2,0:T(8,128)} fusion(f32[16]{0:T(128)S(1)} %get-tuple-element.245, bf16[16,256,768]{2,1,0:T(8,128)(2,1)} %gather_fusion.1, pred[16]{0:T(512)(128)(4,1)S(1)} %get-tuple-element.249, bf16[96,256,128]{2,1,0:T(8,128)(2,1)} %get-tuple-element.281, s32[]{:T(128)S(6)} %select_n.101), kind=kOutput, calls=%fused_computation.5.clone.1 | convolution fusion | flops 810024960 | bytes 13631572 | tf_op jit(solution)/shard_map/while/body/pil,pik->lpk/dot_general | solution.py:39
  285.6 15.1 %scatter_fusion.1 = f32[768,16,128]{2,0,1:T(8,128)} fusion(f32[768,16,128]{2,0,1:T(8,128)} %get-tuple-element.265, s32[16]{0:T(128)S(1)} %get-tuple-element.247, f32[16,768,128]{2,1,0:T(8,128)} %copy.17), kind=kCustom, calls=%fused_computation.3.clone.clone.1 | custom fusion | flops 1572864 | bytes 18874432 | tf_op jit(solution)/shard_map/while/body/scatter-add | solution.py:43
  310.8 17.6 %scatter_fusion = f32[8,256,512]{2,1,0:T(8,128)} fusion(f32[8,256,512]{2,1,0:T(8,128)} %get-tuple-element.264, s32[16]{0:T(128)S(1)} %get-tuple-element.244, f32[16,256,512]{2,1,0:T(8,128)} %broadcast_multiply_fusion.2), kind=kCustom, calls=%fused_computation.2.clone.clone.1 | custom fusion | flops 2097152 | bytes 25165888 | tf_op jit(solution)/shard_map/while/body/scatter-add | solution.py:42
  332.7 7.2 %multiply_bitcast_fusion.2 = f32[16,768,128]{1,2,0:T(8,128)} fusion(f32[16]{0:T(128)S(1)} %get-tuple-element.245, bf16[16,256,768]{2,1,0:T(8,128)(2,1)} %gather_fusion.1, pred[16]{0:T(512)(128)(4,1)S(1)} %get-tuple-element.249, bf16[96,256,128]{2,1,0:T(8,128)(2,1)} %get-tuple-element.281, s32[]{:T(128)S(6)} %select_n.101), kind=kOutput, calls=%fused_computation.5.clone.1 | convolution fusion | flops 810024960 | bytes 13631572 | tf_op jit(solution)/shard_map/while/body/pil,pik->lpk/dot_general | solution.py:39
  346.4 15.1 %scatter_fusion.1 = f32[768,16,128]{2,0,1:T(8,128)} fusion(f32[768,16,128]{2,0,1:T(8,128)} %get-tuple-element.265, s32[16]{0:T(128)S(1)} %get-tuple-element.247, f32[16,768,128]{2,1,0:T(8,128)} %copy.17), kind=kCustom, calls=%fused_computation.3.clone.clone.1 | custom fusion | flops 1572864 | bytes 18874432 | tf_op jit(solution)/shard_map/while/body/scatter-add | solution.py:43
  371.7 18.0 %scatter_fusion = f32[8,256,512]{2,1,0:T(8,128)} fusion(f32[8,256,512]{2,1,0:T(8,128)} %get-tuple-element.264, s32[16]{0:T(128)S(1)} %get-tuple-element.244, f32[16,256,512]{2,1,0:T(8,128)} %broadcast_multiply_fusion.2), kind=kCustom, calls=%fused_computation.2.clone.clone.1 | custom fusion | flops 2097152 | bytes 25165888 | tf_op jit(solution)/shard_map/while/body/scatter-add | solution.py:42
  389.7 112.0 %reduce-scatter.4.cloned.1.call-done = f32[512,512]{1,0:T(8,128)} async-done(((f32[2048,512]{1,0:T(8,128)}), f32[512,512]{1,0:T(8,128)}) %reduce-scatter.4.cloned.1.call-update) | async-done | bytes 1048592 | tf_op jit(solution)/shard_map/reduce_scatter | solution.py:54
  501.8 29.9 %reduce-scatter.6.cloned.1.call-done = f32[128,512]{1,0:T(8,128)} async-done(((f32[512,512]{1,0:T(8,128)}), f32[128,512]{1,0:T(8,128)}) %reduce-scatter.6.cloned.1.call-update) | async-done | bytes 262160 | tf_op jit(solution)/shard_map/reduce_scatter | solution.py:55
  541.2 112.0 %all-reduce.3.cloned.1.call-done = f32[768,512]{1,0:T(8,128)} async-done(((f32[768,512]{1,0:T(8,128)}), f32[768,512]{1,0:T(8,128)}) %all-reduce.3.cloned.1.call-update) | async-done | bytes 1572880 | tf_op jit(solution)/shard_map/psum | solution.py:64
  653.3 17.4 %reduce-scatter.8.cloned.1.call-done = f32[384,2048]{1,0:T(8,128)} async-done(((f32[768,2048]{1,0:T(8,128)}), f32[384,2048]{1,0:T(8,128)}) %reduce-scatter.8.cloned.1.call-update) | async-done | bytes 3145744 | tf_op jit(solution)/shard_map/reduce_scatter | solution.py:56
  674.7 19.7 %all-reduce.5.cloned.1.call-done = f32[768,512]{1,0:T(8,128)} async-done(((f32[768,512]{1,0:T(8,128)}), f32[768,512]{1,0:T(8,128)}) %all-reduce.5.cloned.1.call-update) | async-done | bytes 1572880 | tf_op jit(solution)/shard_map/psum | solution.py:65
  (61 shorter events, 116.9 us)
Async XLA Ops:
  7.2 67.8 %all-gather.2.cloned.1.call-start = ((), (), s32[]{:S(2)}) async-start(), calls=%async_computation.3 | async-start | bytes 3932160 | tf_op jit(solution)/shard_map/all_gather | solution.py:17
  7.9 493.9 %reduce-scatter.4.cloned.1.call-start = ((), (), s32[]{:S(2)}) async-start(), calls=%async_computation.4 | async-start | bytes 5242880 | tf_op jit(solution)/shard_map/reduce_scatter | solution.py:54
  78.1 5.9 copy-start.1
  389.7 142.1 %reduce-scatter.6.cloned.1.call-start = ((), (), s32[]{:S(2)}) async-start(), calls=%async_computation.5 | async-start | bytes 1310720 | tf_op jit(solution)/shard_map/reduce_scatter | solution.py:55
  501.8 151.5 %all-reduce.3.cloned.1.call-start = ((), (), s32[]{:S(2)}) async-start(), calls=%async_computation.7 | async-start | bytes 3145728 | tf_op jit(solution)/shard_map/psum | solution.py:64
  534.7 135.9 %reduce-scatter.8.cloned.1.call-start = ((), (), s32[]{:S(2)}) async-start(), calls=%async_computation.6 | async-start | bytes 9437184 | tf_op jit(solution)/shard_map/reduce_scatter | solution.py:56
  541.2 129.5 %copy-start = (f32[384,2048]{1,0:T(8,128)S(1)}, f32[384,2048]{1,0:T(8,128)}, u32[]{:S(2)}) copy-start(f32[384,2048]{1,0:T(8,128)} %param.13) | copy-start | bytes 9437188
  541.2 153.2 %all-reduce.5.cloned.1.call-start = ((), (), s32[]{:S(2)}) async-start(), calls=%async_computation.8 | async-start | bytes 3145728 | tf_op jit(solution)/shard_map/psum | solution.py:65
Sparse Core Ops, SparseCore 0:
  9.5 65.3 all-gather.1
  389.8 111.9 reduce-scatter.3
  504.6 27.0 reduce-scatter.5
  537.6 115.6 all-reduce.2
  655.4 15.1 reduce-scatter.7
  672.8 21.5 all-reduce.4
